TPU v7x, 256 devices: a whole 4x4x8 slice. The times are simulated.
256 devices in a mesh: gx: 8 (over z), gy: 32 (over y, x, core).
Axes of the slice: x: 4, y: 4, z: 8, core: 2. Of those that a mesh axis runs over, the one named last changes fastest.
Arguments:
- coupling: bfloat16 [8, 256, 1024, 512], P('gx', 'gy'), may hold values from -0.44921875 to 0.44921875
- local_block: bfloat16 [8, 256, 512, 512], P('gx', 'gy'), as said below
- counts: int32 [8, 256], P('gx', 'gy'), may hold values from 1 to 4, as said below
- primal: int32 [8, 256, 512], P('gx', 'gy'), may hold values from 0 to 511
- partner: int32 [3, 8], replicated, may hold values from 0 to 7, as said below
Outputs:
- coarse: float32 [8, 512, 512], P('gx')
Inputs may be any that keep to these rules, and one draw needn't show every extreme that they name: Each row of partner is a perfect matching of the 8 columns: partner[r, partner[r, c]] == c and partner[r, c] != c. `counts`: in each subdomain column at least one subdomain has all 4 blocks live. `primal`: any constraint may hold any number of rows. `local_block`: diagonal entries are positive.
All inputs are finite; a program needn't handle non-finite values. Where the computation divides by a largest or mean magnitude, that divisor is 1e-20 or more.
Results may differ from a plain program's by a relative error of at most 0.00078.
Values sent between devices are 32-bit elements; how exact they have to be, the bound alone decides.
A program may use at most 192 MiB of HBM per device.

v0:
```python
import jax
import jax.numpy as jnp
from jax import lax
from jax.sharding import PartitionSpec as P

BLK = 128
NC = 512
ROUNDS = 3
R = 512


def per_device(coupling, local_block, counts, primal, partner):
    column = lax.axis_index("gx")
    stiff = jnp.diagonal(local_block[0], axis1=1, axis2=2).astype(jnp.float32)
    total = stiff
    for r in range(ROUNDS):
        mate = partner[r, column]
        piece = jax.tree.map(
            lambda part: lax.all_gather(part, "gx", axis=0, tiled=True), stiff[None]
        )
        index = jnp.arange(piece.shape[0], dtype=jnp.int32)
        hit = (index == mate)[:, None, None]
        total = total + (
            jnp.zeros_like(stiff)
            + jnp.sum(jnp.where(hit, piece, jnp.zeros((), jnp.float32)), axis=0)
        )
    weight = stiff / total
    rows = jnp.arange(R, dtype=jnp.int32)
    live = (rows[None, :] < counts[0][:, None] * BLK).astype(jnp.float32)
    gram = jnp.einsum("snr,snq->srq", coupling[0], coupling[0], preferred_element_type=jnp.float32)
    schur = (
        (local_block[0].astype(jnp.float32) - gram) * live[:, :, None] * live[:, None, :]
    ).astype(jnp.bfloat16)
    onehot = primal[0][:, :, None] == jnp.arange(NC, dtype=jnp.int32)[None, None, :]
    basis = jnp.where(onehot, weight[:, :, None], jnp.zeros((), jnp.float32)).astype(jnp.bfloat16)
    image = jnp.einsum("srq,sqk->srk", schur, basis, preferred_element_type=jnp.float32).astype(
        jnp.bfloat16
    )
    tile = jnp.einsum("srk,srl->kl", basis, image, preferred_element_type=jnp.float32)
    summed = lax.psum(tile, "gy")
    scale = 1.0 / jnp.sqrt(jnp.mean(jnp.abs(summed), axis=1) + 1e-06)
    result = summed * scale[:, None] * scale[None, :]
    return result[None]


def solution(mesh):
    placed = (
        P("gx", "gy", None, None),
        P("gx", "gy", None, None),
        P("gx", "gy"),
        P("gx", "gy", None),
        P(),
    )
    return jax.shard_map(
        per_device, mesh=mesh, in_specs=placed, out_specs=P("gx", None, None), check_vma=False
    )
```

profile of v0, /device:TPU:1, one launch (start us, length us, event | category | flops | bytes accessed | tf_op | source)
XLA Modules:
  0.0 238.6 jit_solution(16034111459191862440)
XLA Ops:
  6.5 0.0 all-reduce.2.cloned.1.call-start
  6.5 1.5 constant_dynamic-slice_fusion
  8.0 0.7 iota_compare_fusion.4
  8.7 44.1 %copy.19 = bf16[8,512,512]{0,2,1:T(8,128)(2,1)} copy(bf16[8,512,512]{2,1,0:T(8,128)(2,1)} %bitcast.35) | data formatting | bytes 8388608 | tf_op jit(solution)/shard_map/squeeze | solution.py:14
  52.8 6.5 %gather_fusion = bf16[512,8]{1,0:T(8,128)(2,1)S(1)} fusion(bf16[8,512,512]{0,2,1:T(8,128)(2,1)} %copy.19, s32[512]{0:T(512)S(1)} %bitcast.34), kind=kCustom, calls=%fused_computation | custom fusion | bytes 20480 | tf_op jit(solution)/shard_map/jit(diagonal)/gather | solution.py:14
  59.3 0.1 copy.20
  59.3 23.0 %all-gather = f32[64,512]{1,0:T(8,128)S(1)} all-gather(f32[8,512]{1,0:T(8,128)S(1)} %convert_bitcast_fusion), channel_id=2, replica_groups=mesh['gx'=8,'gy'=32] {'gx'}, dimensions={0}, use_global_device_ids=true | all-gather | bytes 147456 | tf_op jit(solution)/shard_map/all_gather | solution.py:19
  82.4 0.0 copy-start.1
  82.4 0.0 copy-start
  82.4 13.6 %fusion = f32[8,512,512]{2,1,0:T(8,128)} fusion(bf16[1,8,1024,512]{3,2,1,0:T(8,128)(2,1)} %param.5), kind=kOutput, calls=%fused_computation.1 | convolution fusion | flops 4294967296 | bytes 16777216 | tf_op jit(solution)/shard_map/snr,snq->srq/dot_general | solution.py:30
  95.9 0.0 copy-done.1
  95.9 0.1 fusion.21
  96.0 1.2 iota_compare_fusion.2
  97.2 0.1 fusion.18
  97.4 0.0 copy-done
  97.4 10.2 %fusion.15 = f32[512,512]{1,0:T(8,128)} fusion(f32[8,512,512]{2,1,0:T(8,128)} %fusion, f32[8,512]{1,0:T(8,128)S(1)} %fusion.21, bf16[8,512]{1,0:T(8,128)(2,1)S(1)} %add_divide_fusion, s32[8,512]{1,0:T(8,128)S(1)} %bitcast.36, bf16[1,8,512,512]{3,2,1,0:T(8,128)(2,1)} %param.6), kind=kOutput, calls=%fused_computation.14 | convolution fusion | flops 4315938816 | bytes 13672448 | tf_op jit(solution)/shard_map/srk,srl->kl/dot_general | solution.py:39
  107.6 0.0 all-reduce.2.cloned.1.call-update
  107.6 120.4 %all-reduce.2.cloned.1.call-done = f32[512,512]{1,0:T(8,128)} async-done(((f32[512,512]{1,0:T(8,128)}), f32[512,512]{1,0:T(8,128)}) %all-reduce.2.cloned.1.call-update) | async-done | bytes 1048592 | tf_op jit(solution)/shard_map/psum | solution.py:40
  228.0 1.4 abs_reduce_fusion
  229.4 2.4 multiply_bitcast_fusion
  (5 shorter events, 0.0 us)
Async XLA Ops:
  6.5 221.5 %all-reduce.2.cloned.1.call-start = ((), (), s32[]{:S(2)}) async-start(), calls=%async_computation | async-start | bytes 2097152 | tf_op jit(solution)/shard_map/psum | solution.py:40
  82.4 13.6 %copy-start.1 = (s32[1,8]{1,0:T(1,128)S(1)}, s32[1,8]{1,0:T(1,128)}, u32[]{:S(2)}) copy-start(s32[1,8]{1,0:T(1,128)} %param.7) | copy-start | bytes 100
  82.4 15.0 %copy-start = (s32[1,8,512]{2,1,0:T(8,128)S(1)}, s32[1,8,512]{2,1,0:T(8,128)}, u32[]{:S(2)}) copy-start(s32[1,8,512]{2,1,0:T(8,128)} %param.8) | copy-start | bytes 49156
Sparse Core Ops, SparseCore 0:
  107.7 120.2 all-reduce.1
where the time goes:
time: 241 us; the launch traced here: 239 us
  waiting for transfers between devices  120 us (50%)
  local copies, waits for them, and re-layouts  52.1 us (22%)
  matrix products  23.7 us (10%)
  blocking collectives  23 us (10%)
  between operations  13.4 us (6%)
  other arithmetic  5.85 us (2%)
    psum x1, waiting for transfers between devices, per_device(): summed = lax.psum(tile, 'gy')  120 us
    squeeze x1, local copies, waits for them, and re-layouts, per_device(): stiff = jnp.diagonal(local_block[0], axis1=1, axis2=2).astype(jnp.float32)  44.1 us
    all_gather x1, blocking collectives, per_device(): lax.all_gather(part, 'gx', axis=0, tiled=True)  23 us
    dot_general x1, matrix products, per_device(): jnp.einsum('snr,snq->srq', coupling[0], coupling[0], preferred_element_ty...  13.6 us
    dot_general x1, matrix products, per_device(): jnp.einsum('srk,srl->kl', basis, image, preferred_element_type=jnp.float32)  10.2 us
    gather x2, local copies, waits for them, and re-layouts, per_device(): stiff = jnp.diagonal(local_block[0], axis1=1, axis2=2).astype(jnp.float32)  6.53 us
  transfers between devices with their start and end apart: 1, of which 1 were waited for; matrix products, arithmetic and copies ran while one was open for 0% of the time, Pallas kernels for 0%

commit v1 on v0

v1 whole, which is shorter than its diff:
```python
import jax
import jax.numpy as jnp
from jax import lax
from jax.experimental import pallas as pl
from jax.experimental.pallas import tpu as pltpu
from jax.sharding import PartitionSpec as P

BLK = 128
NC = 512
ROUNDS = 3
R = 512
NI = 1024
SUBS = 8
NCOL = 8
SIDE = 4
CHIPS = SIDE * SIDE
CB = 256
CHUNKS = NC // CB
HALF = NC // 2
PIECE = HALF // CHIPS
MESH = pl.DeviceIdType.MESH
F32 = jnp.float32
BF16 = jnp.bfloat16

STEPS = (1, 3, 2)
PLANE = sorted(
    [(dy, dx) for dy in range(SIDE) for dx in range(SIDE) if (dy, dx) != (0, 0)],
    key=lambda o: -(min(o[0], SIDE - o[0]) + min(o[1], SIDE - o[1])),
)
LINE = (4, 3, 5, 2, 6, 1, 7)


def kernel(
    coupling, local_block, counts, primal, partner, out,
    c_v, l_v, s_v, bt, img, stiffs, weight, tile, a_recv, b_recv, full,
    c_sem, l_sem, z_send, z_recv, a_send, a_rsem, b_send, b_rsem, g_send, g_rsem, f_send, f_rsem,
):
    gx = lax.axis_index("gx")
    gy = lax.axis_index("gy")
    core = gy % 2
    x = (gy // 2) % SIDE
    y = gy // (2 * SIDE)
    chip = gy // 2

    def at(dy, dx):
        return ((y + dy) % SIDE) * SIDE + (x + dx) % SIDE

    def on(chip_index, core_index):
        return (gx, chip_index * 2 + core_index)

    sibling = on(chip, 1 - core)
    barrier = pltpu.get_barrier_semaphore()
    for dz in LINE:
        pl.semaphore_signal(barrier, inc=1, device_id=((gx + dz) % NCOL, gy), device_id_type=MESH)
    for dy, dx in PLANE:
        pl.semaphore_signal(barrier, inc=1, device_id=on(at(dy, dx), core), device_id_type=MESH)
    pl.semaphore_signal(barrier, inc=1, device_id=sibling, device_id_type=MESH)

    loads_l = [pltpu.make_async_copy(local_block.at[j], l_v.at[j], l_sem.at[j]) for j in range(SUBS)]
    loads_c = [pltpu.make_async_copy(coupling.at[j], c_v.at[j], c_sem.at[j]) for j in range(SUBS)]
    for load in loads_l:
        load.start()
    for load in loads_c:
        load.start()

    eye = lax.broadcasted_iota(jnp.int32, (BLK, BLK), 0) == lax.broadcasted_iota(
        jnp.int32, (BLK, BLK), 1
    )
    for j in range(SUBS):
        loads_l[j].wait()
        for b in range(R // BLK):
            span = pl.ds(BLK * b, BLK)
            block = l_v[j, span, span].astype(F32)
            stiffs[gx, pl.ds(j, 1), span] = jnp.sum(
                jnp.where(eye, block, 0.0), axis=0, keepdims=True
            )
    pl.semaphore_wait(barrier, len(LINE) + len(PLANE) + 1)
    z_copies = []
    for i, dz in enumerate(LINE):
        z_copies.append(
            pltpu.make_async_remote_copy(
                src_ref=stiffs.at[gx],
                dst_ref=stiffs.at[gx],
                send_sem=z_send.at[i],
                recv_sem=z_recv.at[i],
                device_id=((gx + dz) % NCOL, gy),
                device_id_type=MESH,
            )
        )
        z_copies[-1].start()

    columns = lax.broadcasted_iota(jnp.int32, (1, R), 1)
    for j in range(SUBS):
        loads_c[j].wait()
        c = c_v[j]
        gram = lax.dot_general(c, c, (((0,), (0,)), ((), ())), preferred_element_type=F32)
        count = counts[0, j]
        for b in range(R // BLK):
            span = pl.ds(BLK * b, BLK)
            live = (columns < count * BLK) & (b < count)
            s_v[j, span, :] = jnp.where(
                live, l_v[j, span, :].astype(F32) - gram[BLK * b : BLK * (b + 1)], 0.0
            ).astype(BF16)

    for i, dz in enumerate(LINE):
        there = stiffs.at[(gx + NCOL - dz) % NCOL]
        pltpu.make_async_remote_copy(
            src_ref=there, dst_ref=there, send_sem=z_send.at[i], recv_sem=z_recv.at[i],
            device_id=((gx + dz) % NCOL, gy), device_id_type=MESH,
        ).wait_recv()
    stiff = stiffs[gx]
    total = stiff
    for r in range(ROUNDS):
        total = total + stiffs[partner[r, gx]]
    weight[...] = stiff / total
    constraint = lax.broadcasted_iota(jnp.int32, (NC, R), 0)
    for j in range(SUBS):
        bt[j] = jnp.where(
            constraint == primal[pl.ds(j, 1), :], weight[pl.ds(j, 1), :], 0.0
        ).astype(BF16)

    def images(k):
        for j in range(SUBS):
            img[k, j] = lax.dot_general(
                s_v[j], bt[j, pl.ds(k * CB, CB), :], (((1,), (1,)), ((), ())),
                preferred_element_type=F32,
            ).astype(BF16)

    def tiles(k, first, last, so_far):
        for j in range(first, last):
            term = jnp.dot(bt[j], img[k, j], preferred_element_type=F32)
            so_far = term if so_far is None else so_far + term
        return so_far

    mine = pl.ds(pl.multiple_of(core * HALF, HALF), HALF)
    its = pl.ds(pl.multiple_of((1 - core) * HALF, HALF), HALF)

    def piece(chip_index):
        return pl.ds(pl.multiple_of(core * HALF + chip_index * PIECE, PIECE), PIECE)

    def pair_copy(k):
        return pltpu.make_async_remote_copy(
            src_ref=tile.at[k, its], dst_ref=a_recv.at[k], send_sem=a_send.at[k],
            recv_sem=a_rsem.at[k], device_id=sibling, device_id_type=MESH,
        )

    def scatter_copy(k, i):
        dy, dx = PLANE[i]
        return pltpu.make_async_remote_copy(
            src_ref=tile.at[k, piece(at(dy, dx))], dst_ref=b_recv.at[k, i], send_sem=b_send.at[k, i],
            recv_sem=b_rsem.at[k, i], device_id=on(at(dy, dx), core), device_id_type=MESH,
        )

    def gather_copy(k, i, source):
        dy, dx = PLANE[i]
        return pltpu.make_async_remote_copy(
            src_ref=full.at[k, piece(source)], dst_ref=full.at[k, piece(source)],
            send_sem=g_send.at[k, i], recv_sem=g_rsem.at[k, i],
            device_id=on(at(dy, dx), core), device_id_type=MESH,
        )

    def from_chip(i):
        dy, dx = PLANE[i]
        return at(SIDE - dy, SIDE - dx)

    def forward_copy(k, i, rows):
        return pltpu.make_async_remote_copy(
            src_ref=full.at[k, rows], dst_ref=full.at[k, rows], send_sem=f_send.at[k, i],
            recv_sem=f_rsem.at[k, i], device_id=sibling, device_id_type=MESH,
        )

    def scatter(k):
        pair_copy(k).wait()
        tile[k, mine, :] = tile[k, mine, :] + a_recv[k]
        for i in range(len(PLANE)):
            scatter_copy(k, i).start()

    def reduce_and_gather(k):
        own = tile[k, piece(chip), :]
        for i in range(len(PLANE)):
            scatter_copy(k, i).wait_recv()
            own = own + b_recv[k, i]
        full[k, piece(chip), :] = own
        for i in range(len(PLANE)):
            gather_copy(k, i, chip).start()
        forward_copy(k, len(PLANE), piece(chip)).start()

    near_first = range(len(PLANE) - 1, -1, -1)

    def forward(k):
        for i in near_first:
            gather_copy(k, i, from_chip(i)).wait_recv()
            forward_copy(k, i, piece(from_chip(i))).start()

    images(0)
    tile[0] = tiles(0, 0, SUBS, None)
    pair_copy(0).start()
    images(1)
    part = tiles(1, 0, 6, None)
    scatter(0)
    tile[1] = tiles(1, 6, SUBS, part)
    pair_copy(1).start()
    scatter(1)
    for k in range(CHUNKS):
        reduce_and_gather(k)
    for k in range(CHUNKS):
        forward(k)
    other = 1 - core

    def other_piece(chip_index):
        return pl.ds(pl.multiple_of(other * HALF + chip_index * PIECE, PIECE), PIECE)

    for k in range(CHUNKS):
        for i in near_first:
            forward_copy(k, i, other_piece(from_chip(i))).wait_recv()
        forward_copy(k, len(PLANE), other_piece(chip)).wait_recv()

    size = jnp.sum(jnp.abs(full[0]) + jnp.abs(full[1]), axis=1, keepdims=True)
    scale = 1.0 / jnp.sqrt(size / NC + 1e-06)
    across = [
        jnp.sum(jnp.where(eye, scale[BLK * b : BLK * (b + 1)], 0.0), axis=0, keepdims=True)
        for b in range(NC // BLK)
    ]
    across = jnp.concatenate(across, axis=1)
    for k in range(CHUNKS):
        out[:, pl.ds(k * CB, CB)] = full[k] * scale * across[:, k * CB : (k + 1) * CB]

    for copy in z_copies:
        copy.wait_send()
    for k in range(CHUNKS):
        for i in range(len(PLANE)):
            scatter_copy(k, i).wait_send()
            gather_copy(k, i, chip).wait_send()
            forward_copy(k, i, piece(from_chip(i))).wait_send()
        forward_copy(k, len(PLANE), piece(chip)).wait_send()


def per_device(coupling, local_block, counts, primal, partner):
    dma = pltpu.SemaphoreType.DMA
    peers = len(PLANE)
    result = pl.pallas_call(
        kernel,
        name="coarse",
        out_shape=jax.ShapeDtypeStruct((NC, NC), F32),
        in_specs=[
            pl.BlockSpec(memory_space=pltpu.HBM),
            pl.BlockSpec(memory_space=pltpu.HBM),
            pl.BlockSpec(memory_space=pltpu.SMEM),
            pl.BlockSpec(memory_space=pltpu.VMEM),
            pl.BlockSpec(memory_space=pltpu.SMEM),
        ],
        out_specs=pl.BlockSpec(memory_space=pltpu.VMEM),
        scratch_shapes=[
            pltpu.VMEM((SUBS, NI, R), BF16),
            pltpu.VMEM((SUBS, R, R), BF16),
            pltpu.VMEM((SUBS, R, R), BF16),
            pltpu.VMEM((SUBS, NC, R), BF16),
            pltpu.VMEM((CHUNKS, SUBS, R, CB), BF16),
            pltpu.VMEM((NCOL, SUBS, R), F32),
            pltpu.VMEM((SUBS, R), F32),
            pltpu.VMEM((CHUNKS, NC, CB), F32),
            pltpu.VMEM((CHUNKS, HALF, CB), F32),
            pltpu.VMEM((CHUNKS, peers, PIECE, CB), F32),
            pltpu.VMEM((CHUNKS, NC, CB), F32),
            dma((SUBS,)),
            dma((SUBS,)),
            dma((len(LINE),)),
            dma((len(LINE),)),
            dma((CHUNKS,)),
            dma((CHUNKS,)),
            dma((CHUNKS, peers)),
            dma((CHUNKS, peers)),
            dma((CHUNKS, peers)),
            dma((CHUNKS, peers)),
            dma((CHUNKS, peers + 1)),
            dma((CHUNKS, peers + 1)),
        ],
        compiler_params=pltpu.CompilerParams(
            collective_id=0, has_side_effects=True, vmem_limit_bytes=52 << 20
        ),
    )(coupling[0], local_block[0], counts, primal[0], partner)
    return result[None]


def solution(mesh):
    placed = (
        P("gx", "gy", None, None),
        P("gx", "gy", None, None),
        P("gx", "gy"),
        P("gx", "gy", None),
        P(),
    )
    return jax.shard_map(
        per_device, mesh=mesh, in_specs=placed, out_specs=P("gx", None, None), check_vma=False
    )
```

time: 241 us -> 47.2 us (0.20)
  waiting for transfers between devices: 120 us -> 0 us
  local copies, waits for them, and re-layouts: 52.1 us -> 3.03 us
  Pallas kernels: 0 us -> 44 us
  matrix products: 23.7 us -> 0 us
  blocking collectives: 23 us -> 0 us
  between operations: 13.4 us -> 0.01 us
  other arithmetic: 5.85 us -> 0 us
    psum x1 -> x0, waiting for transfers between devices: 120 us -> none  [per_device(): summed = lax.psum(tile, 'gy')]
    squeeze x1 -> x0, local copies, waits for them, and re-layouts: 44.1 us -> none  [per_device(): stiff = jnp.diagonal(local_block[0], axis1=1, axis2=2).astype(jnp.float32)]
    pallas_call x0 -> x1, Pallas kernels: none -> 44 us  [per_device(): pl.pallas_call(kernel, name='coarse', out_shape=jax.ShapeDtypeStruct((NC,...]
    dot_general x2 -> x0, matrix products: 23.7 us -> none  [the longest x1 13.6 us: per_device(): jnp.einsum('snr,snq->srq', coupling[0], coupling[0], preferred_element_ty...]
    all_gather x1 -> x0, blocking collectives: 23 us -> none  [per_device(): lax.all_gather(part, 'gx', axis=0, tiled=True)]
    gather x2 -> x0, local copies, waits for them, and re-layouts: 6.53 us -> none  [per_device(): stiff = jnp.diagonal(local_block[0], axis1=1, axis2=2).astype(jnp.float32)]
    unnamed x4 -> x7, local copies, waits for them, and re-layouts: 0.01 us -> 3.03 us
  transfers between devices with their start and end apart: 1 -> 0, of which waited for: 1 -> 0; matrix products, arithmetic and copies ran while one was open for 0% -> 0% of each run, Pallas kernels for 0% -> 0%
where the time goes in v1:
time: 47.2 us; the launch traced here: 47 us
  Pallas kernels  44 us (93%)
  local copies, waits for them, and re-layouts  3.03 us (6%)
    pallas_call x1, Pallas kernels, per_device(): pl.pallas_call(kernel, name='coarse', out_shape=jax.ShapeDtypeStruct((NC,...  44 us
    unnamed x7, local copies, waits for them, and re-layouts  3.03 us

profile of v1, /device:TPU:1, one launch (start us, length us, event | category | flops | bytes accessed | tf_op | source)
XLA Modules:
  0.0 47.0 jit_solution(10303329646127052200)
XLA Ops:
  0.0 0.0 copy-start
  0.0 0.7 %copy-done = s32[1,8,512]{2,1,0:T(8,128)S(1)} copy-done((s32[1,8,512]{2,1,0:T(8,128)S(1)}, s32[1,8,512]{2,1,0:T(8,128)}, u32[]{:S(2)}) %copy-start) | copy-done | bytes 16408
  0.7 0.0 copy-start.1
  0.7 0.7 %copy-done.1 = s32[3,8]{1,0:T(4,128)S(1)} copy-done((s32[3,8]{1,0:T(4,128)S(1)}, s32[3,8]{1,0:T(4,128)}, u32[]{:S(2)}) %copy-start.1) | copy-done | bytes 120
  1.4 0.0 copy-start.2
  1.4 0.7 %copy-done.2 = s32[1,8]{1,0:T(1,128)S(1)} copy-done((s32[1,8]{1,0:T(1,128)S(1)}, s32[1,8]{1,0:T(1,128)}, u32[]{:S(2)}) %copy-start.2) | copy-done | bytes 56
  2.1 44.0 %coarse.1 = f32[512,512]{1,0:T(8,128)S(1)} custom-call(bf16[8,1024,512]{2,1,0:T(8,128)(2,1)} %bitcast.6, bf16[8,512,512]{2,1,0:T(8,128)(2,1)} %bitcast.7, s32[1,8]{1,0:T(1,128)S(1)} %copy-done.2, s32[8,512]{1,0:T(8,128)S(1)} %bitcast.5, s32[3,8]{1,0:T(4,128)S(1)} %copy-done.1), custom_call_target="tpu_custom_call" | custom-call | tf_op jit(solution)/shard_map/coarse/pallas_call | solution.py:241
  46.0 1.0 %copy.7 = f32[1,512,512]{2,1,0:T(8,128)} copy(f32[1,512,512]{2,1,0:T(8,128)S(1)} %bitcast.4) | data formatting | bytes 2097152
Async XLA Ops:
  0.0 0.7 %copy-start = (s32[1,8,512]{2,1,0:T(8,128)S(1)}, s32[1,8,512]{2,1,0:T(8,128)}, u32[]{:S(2)}) copy-start(s32[1,8,512]{2,1,0:T(8,128)} %param.8) | copy-start | bytes 49156
  0.7 0.7 %copy-start.1 = (s32[3,8]{1,0:T(4,128)S(1)}, s32[3,8]{1,0:T(4,128)}, u32[]{:S(2)}) copy-start(s32[3,8]{1,0:T(4,128)} %partner.1) | copy-start | bytes 292
  1.4 0.7 %copy-start.2 = (s32[1,8]{1,0:T(1,128)S(1)}, s32[1,8]{1,0:T(1,128)}, u32[]{:S(2)}) copy-start(s32[1,8]{1,0:T(1,128)} %counts.1) | copy-start | bytes 100

commit v2 on v1

--- a/solution.py
+++ b/solution.py
@@ -32,8 +32,8 @@
 
 def kernel(
     coupling, local_block, counts, primal, partner, out,
-    c_v, l_v, s_v, bt, img, stiffs, weight, tile, a_recv, b_recv, full,
-    c_sem, l_sem, z_send, z_recv, a_send, a_rsem, b_send, b_rsem, g_send, g_rsem, f_send, f_rsem,
+    c_v, l_v, d_v, p_v, count_s, partner_s, s_v, bt, img, stiffs, weight, tile, a_recv, b_recv, full,
+    c_sem, l_sem, d_sem, o_sem, z_send, z_recv, a_send, a_rsem, b_send, b_rsem, g_send, g_rsem, f_send, f_rsem,
 ):
     gx = lax.axis_index("gx")
     gy = lax.axis_index("gy")
@@ -48,6 +48,28 @@
     def on(chip_index, core_index):
         return (gx, chip_index * 2 + core_index)
 
+    def loads(j):
+        return (
+            pltpu.make_async_copy(coupling.at[j], c_v.at[j], c_sem.at[j]),
+            pltpu.make_async_copy(local_block.at[j], l_v.at[j], l_sem.at[j]),
+        )
+
+    def spans(b):
+        return pl.ds(BLK * b, BLK)
+
+    diagonal = [
+        pltpu.make_async_copy(
+            local_block.at[:, spans(b), spans(b)], d_v.at[b], d_sem.at[b]
+        )
+        for b in range(R // BLK)
+    ]
+    small = [
+        pltpu.make_async_copy(primal, p_v, o_sem.at[0]),
+        pltpu.make_async_copy(counts, count_s, o_sem.at[1]),
+        pltpu.make_async_copy(partner, partner_s, o_sem.at[2]),
+    ]
+    for load in diagonal + small:
+        load.start()
     sibling = on(chip, 1 - core)
     barrier = pltpu.get_barrier_semaphore()
     for dz in LINE:
@@ -56,24 +78,21 @@
         pl.semaphore_signal(barrier, inc=1, device_id=on(at(dy, dx), core), device_id_type=MESH)
     pl.semaphore_signal(barrier, inc=1, device_id=sibling, device_id_type=MESH)
 
-    loads_l = [pltpu.make_async_copy(local_block.at[j], l_v.at[j], l_sem.at[j]) for j in range(SUBS)]
-    loads_c = [pltpu.make_async_copy(coupling.at[j], c_v.at[j], c_sem.at[j]) for j in range(SUBS)]
-    for load in loads_l:
-        load.start()
-    for load in loads_c:
-        load.start()
+    for j in range(SUBS):
+        for load in loads(j):
+            load.start()
 
     eye = lax.broadcasted_iota(jnp.int32, (BLK, BLK), 0) == lax.broadcasted_iota(
         jnp.int32, (BLK, BLK), 1
     )
-    for j in range(SUBS):
-        loads_l[j].wait()
-        for b in range(R // BLK):
-            span = pl.ds(BLK * b, BLK)
-            block = l_v[j, span, span].astype(F32)
-            stiffs[gx, pl.ds(j, 1), span] = jnp.sum(
-                jnp.where(eye, block, 0.0), axis=0, keepdims=True
+    for load in diagonal + small:
+        load.wait()
+    for b in range(R // BLK):
+        for j in range(SUBS):
+            stiffs[gx, pl.ds(j, 1), spans(b)] = jnp.sum(
+                jnp.where(eye, d_v[b, j].astype(F32), 0.0), axis=0, keepdims=True
             )
+
     pl.semaphore_wait(barrier, len(LINE) + len(PLANE) + 1)
     z_copies = []
     for i, dz in enumerate(LINE):
@@ -90,17 +109,31 @@
         z_copies[-1].start()
 
     columns = lax.broadcasted_iota(jnp.int32, (1, R), 1)
-    for j in range(SUBS):
-        loads_c[j].wait()
-        c = c_v[j]
-        gram = lax.dot_general(c, c, (((0,), (0,)), ((), ())), preferred_element_type=F32)
-        count = counts[0, j]
-        for b in range(R // BLK):
-            span = pl.ds(BLK * b, BLK)
-            live = (columns < count * BLK) & (b < count)
-            s_v[j, span, :] = jnp.where(
-                live, l_v[j, span, :].astype(F32) - gram[BLK * b : BLK * (b + 1)], 0.0
-            ).astype(BF16)
+
+    def over_rows(a, b):
+        return lax.dot_general(a, b, (((0,), (0,)), ((), ())), preferred_element_type=F32)
+
+    def schur(first, last):
+        for j in range(first, last):
+            for load in loads(j):
+                load.wait()
+        for j in range(first, last):
+            low, high = c_v[j, :, pl.ds(0, R // 2)], c_v[j, :, pl.ds(R // 2, R // 2)]
+            corner = over_rows(low, high)
+            upper = jnp.concatenate([over_rows(low, low), corner], axis=1)
+            lower = jnp.concatenate([corner.T, over_rows(high, high)], axis=1)
+            count = count_s[0, j]
+            for b in range(R // BLK):
+                live = (columns < count * BLK) & (b < count)
+                at_row = BLK * b % (R // 2)
+                gram = (upper if 2 * b < R // BLK else lower)[at_row : at_row + BLK]
+                s_v[j, spans(b), :] = jnp.where(
+                    live, l_v[j, spans(b), :].astype(F32) - gram, 0.0
+                ).astype(BF16)
+
+    schur(0, 1)
+    schur(1, 3)
+    schur(3, SUBS)
 
     for i, dz in enumerate(LINE):
         there = stiffs.at[(gx + NCOL - dz) % NCOL]
@@ -111,12 +144,12 @@
     stiff = stiffs[gx]
     total = stiff
     for r in range(ROUNDS):
-        total = total + stiffs[partner[r, gx]]
+        total = total + stiffs[partner_s[r, gx]]
     weight[...] = stiff / total
     constraint = lax.broadcasted_iota(jnp.int32, (NC, R), 0)
     for j in range(SUBS):
         bt[j] = jnp.where(
-            constraint == primal[pl.ds(j, 1), :], weight[pl.ds(j, 1), :], 0.0
+            constraint == p_v[pl.ds(j, 1), :], weight[pl.ds(j, 1), :], 0.0
         ).astype(BF16)
 
     def images(k):
@@ -126,11 +159,12 @@
                 preferred_element_type=F32,
             ).astype(BF16)
 
-    def tiles(k, first, last, so_far):
-        for j in range(first, last):
-            term = jnp.dot(bt[j], img[k, j], preferred_element_type=F32)
+    def half_tile(k, rows):
+        so_far = None
+        for j in range(SUBS):
+            term = jnp.dot(bt[j, rows, :], img[k, j], preferred_element_type=F32)
             so_far = term if so_far is None else so_far + term
-        return so_far
+        tile[k, rows, :] = so_far
 
     mine = pl.ds(pl.multiple_of(core * HALF, HALF), HALF)
     its = pl.ds(pl.multiple_of((1 - core) * HALF, HALF), HALF)
@@ -193,13 +227,14 @@
             forward_copy(k, i, piece(from_chip(i))).start()
 
     images(0)
-    tile[0] = tiles(0, 0, SUBS, None)
+    half_tile(0, its)
     pair_copy(0).start()
+    half_tile(0, mine)
     images(1)
-    part = tiles(1, 0, 6, None)
     scatter(0)
-    tile[1] = tiles(1, 6, SUBS, part)
+    half_tile(1, its)
     pair_copy(1).start()
+    half_tile(1, mine)
     scatter(1)
     for k in range(CHUNKS):
         reduce_and_gather(k)
@@ -210,12 +245,13 @@
     def other_piece(chip_index):
         return pl.ds(pl.multiple_of(other * HALF + chip_index * PIECE, PIECE), PIECE)
 
+    size = 0.0
     for k in range(CHUNKS):
         for i in near_first:
             forward_copy(k, i, other_piece(from_chip(i))).wait_recv()
         forward_copy(k, len(PLANE), other_piece(chip)).wait_recv()
-
-    size = jnp.sum(jnp.abs(full[0]) + jnp.abs(full[1]), axis=1, keepdims=True)
+        size = size + jnp.sum(jnp.abs(full[k]), axis=1, keepdims=True)
+
     scale = 1.0 / jnp.sqrt(size / NC + 1e-06)
     across = [
         jnp.sum(jnp.where(eye, scale[BLK * b : BLK * (b + 1)], 0.0), axis=0, keepdims=True)
@@ -233,6 +269,10 @@
             gather_copy(k, i, chip).wait_send()
             forward_copy(k, i, piece(from_chip(i))).wait_send()
         forward_copy(k, len(PLANE), piece(chip)).wait_send()
+
+
+def in_hbm(x):
+    return pltpu.with_memory_space_constraint(x, pltpu.HBM)
 
 
 def per_device(coupling, local_block, counts, primal, partner):
@@ -245,14 +285,18 @@
         in_specs=[
             pl.BlockSpec(memory_space=pltpu.HBM),
             pl.BlockSpec(memory_space=pltpu.HBM),
-            pl.BlockSpec(memory_space=pltpu.SMEM),
-            pl.BlockSpec(memory_space=pltpu.VMEM),
-            pl.BlockSpec(memory_space=pltpu.SMEM),
+            pl.BlockSpec(memory_space=pltpu.HBM),
+            pl.BlockSpec(memory_space=pltpu.HBM),
+            pl.BlockSpec(memory_space=pltpu.HBM),
         ],
         out_specs=pl.BlockSpec(memory_space=pltpu.VMEM),
         scratch_shapes=[
             pltpu.VMEM((SUBS, NI, R), BF16),
             pltpu.VMEM((SUBS, R, R), BF16),
+            pltpu.VMEM((R // BLK, SUBS, BLK, BLK), BF16),
+            pltpu.VMEM((SUBS, R), jnp.int32),
+            pltpu.SMEM((1, SUBS), jnp.int32),
+            pltpu.SMEM((ROUNDS, NCOL), jnp.int32),
             pltpu.VMEM((SUBS, R, R), BF16),
             pltpu.VMEM((SUBS, NC, R), BF16),
             pltpu.VMEM((CHUNKS, SUBS, R, CB), BF16),
@@ -264,6 +308,8 @@
             pltpu.VMEM((CHUNKS, NC, CB), F32),
             dma((SUBS,)),
             dma((SUBS,)),
+            dma((R // BLK,)),
+            dma((3,)),
             dma((len(LINE),)),
             dma((len(LINE),)),
             dma((CHUNKS,)),
@@ -278,7 +324,7 @@
         compiler_params=pltpu.CompilerParams(
             collective_id=0, has_side_effects=True, vmem_limit_bytes=52 << 20
         ),
-    )(coupling[0], local_block[0], counts, primal[0], partner)
+    )(coupling[0], local_block[0], *(in_hbm(x) for x in (counts, primal[0], partner)))
     return result[None]
 
 

time: 47.2 us -> 40.7 us (0.86)
  Pallas kernels: 44 us -> 39.6 us
  local copies, waits for them, and re-layouts: 3.03 us -> 0.97 us
    pallas_call x1, Pallas kernels: 44 us -> 39.6 us  [per_device(): pl.pallas_call(kernel, name='coarse', out_shape=jax.ShapeDtypeStruct((NC,...]
    unnamed x7 -> x1, local copies, waits for them, and re-layouts: 3.03 us -> 0.97 us
where the time goes in v2:
time: 40.7 us; the launch traced here: 40.6 us
  Pallas kernels  39.6 us (97%)
  local copies, waits for them, and re-layouts  0.97 us (2%)
    pallas_call x1, Pallas kernels, per_device(): pl.pallas_call(kernel, name='coarse', out_shape=jax.ShapeDtypeStruct((NC,...  39.6 us
    unnamed x1, local copies, waits for them, and re-layouts  0.97 us

profile of v2, /device:TPU:1, one launch (start us, length us, event | category | flops | bytes accessed | tf_op | source)
XLA Modules:
  0.0 40.6 jit_solution(17128758614244902414)
XLA Ops:
  0.0 39.6 %coarse.1 = f32[512,512]{1,0:T(8,128)S(1)} custom-call(bf16[8,1024,512]{2,1,0:T(8,128)(2,1)} %bitcast.5, bf16[8,512,512]{2,1,0:T(8,128)(2,1)} %bitcast.6, s32[1,8]{1,0:T(1,128)} %counts.1, s32[8,512]{1,0:T(8,128)} %bitcast.7, s32[3,8]{1,0:T(4,128)} %partner.1), custom_call_target="tpu_custom_call" | custom-call | tf_op jit(solution)/shard_map/coarse/pallas_call | solution.py:281
  39.6 1.0 %copy.7 = f32[1,512,512]{2,1,0:T(8,128)} copy(f32[1,512,512]{2,1,0:T(8,128)S(1)} %bitcast.4) | data formatting | bytes 2097152

commit v3 on v2

--- a/solution.py
+++ b/solution.py
@@ -32,7 +32,7 @@
 
 def kernel(
     coupling, local_block, counts, primal, partner, out,
-    c_v, l_v, d_v, p_v, count_s, partner_s, s_v, bt, img, stiffs, weight, tile, a_recv, b_recv, full,
+    c_v, l_v, d_v, p_v, count_s, partner_s, s_v, bt, img, stiffs, weight, tile, a_recv, b_recv, full, sums,
     c_sem, l_sem, d_sem, o_sem, z_send, z_recv, a_send, a_rsem, b_send, b_rsem, g_send, g_rsem, f_send, f_rsem,
 ):
     gx = lax.axis_index("gx")
@@ -133,7 +133,8 @@
 
     schur(0, 1)
     schur(1, 3)
-    schur(3, SUBS)
+    schur(3, 5)
+    schur(5, SUBS)
 
     for i, dz in enumerate(LINE):
         there = stiffs.at[(gx + NCOL - dz) % NCOL]
@@ -226,6 +227,15 @@
             gather_copy(k, i, from_chip(i)).wait_recv()
             forward_copy(k, i, piece(from_chip(i))).start()
 
+    def note(k, rows):
+        size = jnp.abs(full[k, rows, pl.ds(0, BLK)]) + jnp.abs(full[k, rows, pl.ds(BLK, BLK)])
+        sums[rows, :] = size if k == 0 else sums[rows, :] + size
+
+    other = 1 - core
+
+    def other_piece(chip_index, count=1):
+        return pl.ds(pl.multiple_of(other * HALF + chip_index * PIECE, PIECE), count * PIECE)
+
     images(0)
     half_tile(0, its)
     pair_copy(0).start()
@@ -240,26 +250,28 @@
         reduce_and_gather(k)
     for k in range(CHUNKS):
         forward(k)
-    other = 1 - core
-
-    def other_piece(chip_index):
-        return pl.ds(pl.multiple_of(other * HALF + chip_index * PIECE, PIECE), PIECE)
-
-    size = 0.0
-    for k in range(CHUNKS):
-        for i in near_first:
-            forward_copy(k, i, other_piece(from_chip(i))).wait_recv()
-        forward_copy(k, len(PLANE), other_piece(chip)).wait_recv()
-        size = size + jnp.sum(jnp.abs(full[k]), axis=1, keepdims=True)
-
-    scale = 1.0 / jnp.sqrt(size / NC + 1e-06)
-    across = [
-        jnp.sum(jnp.where(eye, scale[BLK * b : BLK * (b + 1)], 0.0), axis=0, keepdims=True)
-        for b in range(NC // BLK)
-    ]
-    across = jnp.concatenate(across, axis=1)
-    for k in range(CHUNKS):
-        out[:, pl.ds(k * CB, CB)] = full[k] * scale * across[:, k * CB : (k + 1) * CB]
+        note(k, mine)
+    for k in range(CHUNKS):
+        for dy in (0, 1, 3, 2):
+            if dy == 0:
+                forward_copy(k, len(PLANE), other_piece(chip)).wait_recv()
+            for i in near_first:
+                if (SIDE - PLANE[i][0]) % SIDE == dy:
+                    forward_copy(k, i, other_piece(from_chip(i))).wait_recv()
+            note(k, other_piece(((y + dy) % SIDE) * SIDE, SIDE))
+
+    across, down = [], []
+    for b in range(NC // BLK):
+        size = jnp.sum(sums[spans(b), :].T, axis=0, keepdims=True)
+        scale = 1.0 / jnp.sqrt(size / NC + 1e-06)
+        across.append(scale)
+        down.append(jnp.broadcast_to(scale, (BLK, BLK)).T)
+    for k in range(CHUNKS):
+        for b in range(NC // BLK):
+            for h in range(CB // BLK):
+                out[spans(b), pl.ds(k * CB + h * BLK, BLK)] = (
+                    full[k, spans(b), pl.ds(h * BLK, BLK)] * down[b] * across[k * (CB // BLK) + h]
+                )
 
     for copy in z_copies:
         copy.wait_send()
@@ -306,6 +318,7 @@
             pltpu.VMEM((CHUNKS, HALF, CB), F32),
             pltpu.VMEM((CHUNKS, peers, PIECE, CB), F32),
             pltpu.VMEM((CHUNKS, NC, CB), F32),
+            pltpu.VMEM((NC, BLK), F32),
             dma((SUBS,)),
             dma((SUBS,)),
             dma((R // BLK,)),

time: 40.7 us -> 40.6 us (level)
  no operation moved by 1% of the time
where the time goes in v3:
time: 40.6 us; the launch traced here: 40.5 us
  Pallas kernels  39.6 us (98%)
  local copies, waits for them, and re-layouts  0.97 us (2%)
    pallas_call x1, Pallas kernels, per_device(): pl.pallas_call(kernel, name='coarse', out_shape=jax.ShapeDtypeStruct((NC,...  39.6 us
    unnamed x1, local copies, waits for them, and re-layouts  0.97 us

profile of v3, /device:TPU:1, one launch (start us, length us, event | category | flops | bytes accessed | tf_op | source)
XLA Modules:
  0.0 40.5 jit_solution(8173234557547602190)
XLA Ops:
  0.0 39.6 %coarse.1 = f32[512,512]{1,0:T(8,128)S(1)} custom-call(bf16[8,1024,512]{2,1,0:T(8,128)(2,1)} %bitcast.5, bf16[8,512,512]{2,1,0:T(8,128)(2,1)} %bitcast.6, s32[1,8]{1,0:T(1,128)} %counts.1, s32[8,512]{1,0:T(8,128)} %bitcast.7, s32[3,8]{1,0:T(4,128)} %partner.1), custom_call_target="tpu_custom_call" | custom-call | tf_op jit(solution)/shard_map/coarse/pallas_call | solution.py:293
  39.6 1.0 %copy.7 = f32[1,512,512]{2,1,0:T(8,128)} copy(f32[1,512,512]{2,1,0:T(8,128)S(1)} %bitcast.4) | data formatting | bytes 2097152

commit v4 on v3

--- a/solution.py
+++ b/solution.py
@@ -11,6 +11,7 @@
 R = 512
 NI = 1024
 SUBS = 8
+PART = SUBS // 2
 NCOL = 8
 SIDE = 4
 CHIPS = SIDE * SIDE
@@ -32,7 +33,7 @@
 
 def kernel(
     coupling, local_block, counts, primal, partner, out,
-    c_v, l_v, d_v, p_v, count_s, partner_s, s_v, bt, img, stiffs, weight, tile, a_recv, b_recv, full, sums,
+    c_v, l_v, d_v, p_v, count_s, partner_s, s_v, bt, img, stiffs_a, stiffs_b, weight, tile, a_recv, b_recv, full, sums,
     c_sem, l_sem, d_sem, o_sem, z_send, z_recv, a_send, a_rsem, b_send, b_rsem, g_send, g_rsem, f_send, f_rsem,
 ):
     gx = lax.axis_index("gx")
@@ -87,26 +88,29 @@
     )
     for load in diagonal + small:
         load.wait()
+    stiffs = (stiffs_a, stiffs_b)
     for b in range(R // BLK):
         for j in range(SUBS):
-            stiffs[gx, pl.ds(j, 1), spans(b)] = jnp.sum(
+            row = 2 * (j % PART) + 2 * b // (R // BLK)
+            stiffs[j // PART][gx, pl.ds(row, 1), pl.ds(BLK * b % (R // 2), BLK)] = jnp.sum(
                 jnp.where(eye, d_v[b, j].astype(F32), 0.0), axis=0, keepdims=True
             )
 
     pl.semaphore_wait(barrier, len(LINE) + len(PLANE) + 1)
-    z_copies = []
-    for i, dz in enumerate(LINE):
-        z_copies.append(
-            pltpu.make_async_remote_copy(
-                src_ref=stiffs.at[gx],
-                dst_ref=stiffs.at[gx],
-                send_sem=z_send.at[i],
-                recv_sem=z_recv.at[i],
-                device_id=((gx + dz) % NCOL, gy),
-                device_id_type=MESH,
-            )
-        )
-        z_copies[-1].start()
+
+    def z_copy(h, i, source):
+        return pltpu.make_async_remote_copy(
+            src_ref=stiffs[h].at[source],
+            dst_ref=stiffs[h].at[source],
+            send_sem=z_send.at[h, i],
+            recv_sem=z_recv.at[h, i],
+            device_id=((gx + LINE[i]) % NCOL, gy),
+            device_id_type=MESH,
+        )
+
+    for h in range(2):
+        for i in range(len(LINE)):
+            z_copy(h, i, gx).start()
 
     columns = lax.broadcasted_iota(jnp.int32, (1, R), 1)
 
@@ -136,25 +140,25 @@
     schur(3, 5)
     schur(5, SUBS)
 
-    for i, dz in enumerate(LINE):
-        there = stiffs.at[(gx + NCOL - dz) % NCOL]
-        pltpu.make_async_remote_copy(
-            src_ref=there, dst_ref=there, send_sem=z_send.at[i], recv_sem=z_recv.at[i],
-            device_id=((gx + dz) % NCOL, gy), device_id_type=MESH,
-        ).wait_recv()
-    stiff = stiffs[gx]
-    total = stiff
-    for r in range(ROUNDS):
-        total = total + stiffs[partner_s[r, gx]]
-    weight[...] = stiff / total
     constraint = lax.broadcasted_iota(jnp.int32, (NC, R), 0)
-    for j in range(SUBS):
-        bt[j] = jnp.where(
-            constraint == p_v[pl.ds(j, 1), :], weight[pl.ds(j, 1), :], 0.0
-        ).astype(BF16)
-
-    def images(k):
-        for j in range(SUBS):
+
+    def bases(h):
+        for i, dz in enumerate(LINE):
+            z_copy(h, i, (gx + NCOL - dz) % NCOL).wait_recv()
+        stiff = stiffs[h][gx]
+        total = stiff
+        for r in range(ROUNDS):
+            total = total + stiffs[h][partner_s[r, gx]]
+        weight[h] = stiff / total
+        for q in range(PART):
+            row = jnp.concatenate(
+                [weight[h, pl.ds(2 * q, 1), :], weight[h, pl.ds(2 * q + 1, 1), :]], axis=1
+            )
+            j = h * PART + q
+            bt[j] = jnp.where(constraint == p_v[pl.ds(j, 1), :], row, 0.0).astype(BF16)
+
+    def images(k, first, last):
+        for j in range(first, last):
             img[k, j] = lax.dot_general(
                 s_v[j], bt[j, pl.ds(k * CB, CB), :], (((1,), (1,)), ((), ())),
                 preferred_element_type=F32,
@@ -223,7 +227,7 @@
     near_first = range(len(PLANE) - 1, -1, -1)
 
     def forward(k):
-        for i in near_first:
+        for i in range(len(PLANE)):
             gather_copy(k, i, from_chip(i)).wait_recv()
             forward_copy(k, i, piece(from_chip(i))).start()
 
@@ -236,11 +240,14 @@
     def other_piece(chip_index, count=1):
         return pl.ds(pl.multiple_of(other * HALF + chip_index * PIECE, PIECE), count * PIECE)
 
-    images(0)
+    bases(0)
+    images(0, 0, PART)
+    bases(1)
+    images(0, PART, SUBS)
     half_tile(0, its)
     pair_copy(0).start()
     half_tile(0, mine)
-    images(1)
+    images(1, 0, SUBS)
     scatter(0)
     half_tile(1, its)
     pair_copy(1).start()
@@ -273,8 +280,9 @@
                     full[k, spans(b), pl.ds(h * BLK, BLK)] * down[b] * across[k * (CB // BLK) + h]
                 )
 
-    for copy in z_copies:
-        copy.wait_send()
+    for h in range(2):
+        for i in range(len(LINE)):
+            z_copy(h, i, gx).wait_send()
     for k in range(CHUNKS):
         for i in range(len(PLANE)):
             scatter_copy(k, i).wait_send()
@@ -312,8 +320,9 @@
             pltpu.VMEM((SUBS, R, R), BF16),
             pltpu.VMEM((SUBS, NC, R), BF16),
             pltpu.VMEM((CHUNKS, SUBS, R, CB), BF16),
-            pltpu.VMEM((NCOL, SUBS, R), F32),
-            pltpu.VMEM((SUBS, R), F32),
+            pltpu.VMEM((NCOL, 2 * PART, R // 2), F32),
+            pltpu.VMEM((NCOL, 2 * PART, R // 2), F32),
+            pltpu.VMEM((2, 2 * PART, R // 2), F32),
             pltpu.VMEM((CHUNKS, NC, CB), F32),
             pltpu.VMEM((CHUNKS, HALF, CB), F32),
             pltpu.VMEM((CHUNKS, peers, PIECE, CB), F32),
@@ -323,8 +332,8 @@
             dma((SUBS,)),
             dma((R // BLK,)),
             dma((3,)),
-            dma((len(LINE),)),
-            dma((len(LINE),)),
+            dma((2, len(LINE))),
+            dma((2, len(LINE))),
             dma((CHUNKS,)),
             dma((CHUNKS,)),
             dma((CHUNKS, peers)),

time: 40.6 us -> 40.8 us (level)
  no operation moved by 1% of the time
where the time goes in v4:
time: 40.8 us; the launch traced here: 40.7 us
  Pallas kernels  39.7 us (97%)
  local copies, waits for them, and re-layouts  0.97 us (2%)
    pallas_call x1, Pallas kernels, per_device(): pl.pallas_call(kernel, name='coarse', out_shape=jax.ShapeDtypeStruct((NC,...  39.7 us
    unnamed x1, local copies, waits for them, and re-layouts  0.97 us

profile of v4, /device:TPU:1, one launch (start us, length us, event | category | flops | bytes accessed | tf_op | source)
XLA Modules:
  0.0 40.7 jit_solution(3779414933339793098)
XLA Ops:
  0.0 39.7 %coarse.1 = f32[512,512]{1,0:T(8,128)S(1)} custom-call(bf16[8,1024,512]{2,1,0:T(8,128)(2,1)} %bitcast.5, bf16[8,512,512]{2,1,0:T(8,128)(2,1)} %bitcast.6, s32[1,8]{1,0:T(1,128)} %counts.1, s32[8,512]{1,0:T(8,128)} %bitcast.7, s32[3,8]{1,0:T(4,128)} %partner.1), custom_call_target="tpu_custom_call" | custom-call | tf_op jit(solution)/shard_map/coarse/pallas_call | solution.py:301
  39.7 1.0 %copy.7 = f32[1,512,512]{2,1,0:T(8,128)} copy(f32[1,512,512]{2,1,0:T(8,128)S(1)} %bitcast.4) | data formatting | bytes 2097152
